TPU v7x, 32 devices: a whole 2x2x4 slice. The times are simulated.
32 devices in a mesh: cuts: 2 (over x), rows: 16 (over z, y, core).
Axes of the slice: x: 2, y: 2, z: 4, core: 2. Of those that a mesh axis runs over, the one named last changes fastest.
Arguments:
- start_modes: float32 [2, 64, 512, 128], P('cuts', 'rows'), may hold values from -6 to 6
- contrast: float32 [2, 64, 512], P('cuts', 'rows'), may hold values from 0 to 1
- rotations: float32 [2, 2, 128, 128], P('cuts'), may hold values from -0.2 to 1.2, as said below
- ordering: int32 [2, 2, 128], P('cuts'), may hold values from 0 to 127, each once within a row
Outputs:
- modes: float32 [2, 64, 512, 128], P('cuts', 'rows')
- coupling: float32 [2, 128, 128], P('cuts', 'rows')
- rayleigh: float32 [2, 128, 128], P('cuts', 'rows')
Inputs may be any that keep to these rules, and one draw needn't show every extreme that they name: `rotations`: each matrix is invertible.
All inputs are finite; a program needn't handle non-finite values.
Results may differ from a plain program's by a relative error of at most 0.00026.
Values sent between devices are 32-bit elements; how exact they have to be, the bound alone decides.
No kernel may reach another device: no remote copies, remote signals or barrier semaphores. Data moves between devices by JAX's collectives and lax.ppermute only.
A program may use at most 64 MiB of HBM per device.

v0:
```python
import jax
import jax.numpy as jnp
from jax import lax
from jax.sharding import PartitionSpec as P

DEGREE = 4
ITERS = 2


def padded_2(block, sides, width):
    for axis, dim in sides:
        count = lax.axis_size(axis)
        forward = [(i, i + 1) for i in range(count - 1)]
        backward = [(target, source) for source, target in forward]
        low = lax.ppermute(
            lax.slice_in_dim(block, block.shape[dim] - width, None, axis=dim), axis, forward
        )
        high = lax.ppermute(lax.slice_in_dim(block, 0, width, axis=dim), axis, backward)
        block = jnp.concatenate([low, block, high], axis=dim)
    return block


def from_behind(value, axis, by):
    peers = lax.axis_size(axis)
    pairs = [(i, i + by) for i in range(peers) if 0 <= i + by < peers]
    return lax.ppermute(value, axis, pairs)


def neighbour_sum(center, rows_source):
    columns = jnp.pad(center, ((0, 0), (1, 1), (0, 0)))
    return rows_source[2:] + rows_source[:-2] + columns[:, 2:] + columns[:, :-2]


def operator_core(center, rows_source, section):
    return (
        0.8 * (section[:, :, None] * center + 0.25 * neighbour_sum(center, rows_source))
        - 0.2 * center
    )


def inner_modes(left, right):
    return jnp.einsum("rcm,rcn->mn", left, right, precision=lax.Precision.HIGHEST)


def apply_edge(vectors, section):
    padded = padded_2(vectors, (("rows", 0),), 1)
    return operator_core(vectors, padded, section)


def body(start_modes, contrast, rotations, ordering):
    subspace = start_modes[0]
    section = contrast[0]
    turnings = rotations[0]
    sequence = ordering[0]
    rows_here = subspace.shape[0]
    columns = subspace.shape[1]
    nmodes = subspace.shape[2]
    tiles = lax.axis_size("rows")
    pixels = rows_here * tiles * columns
    wide_section = padded_2(section, (("rows", 0),), DEGREE)
    global_row = (
        lax.axis_index("rows") * rows_here
        + jnp.arange(rows_here + 2 * DEGREE, dtype=jnp.int32)
        - DEGREE
    )
    inside = ((global_row >= 0) & (global_row < rows_here * tiles)).astype(jnp.float32)[
        :, None, None
    ]
    for sweep in range(ITERS):

        def apply_local(vectors):
            return (
                operator_core(vectors, jnp.pad(vectors, ((1, 1), (0, 0), (0, 0))), wide_section)
                * inside
            )

        before = padded_2(subspace, (("rows", 0),), DEGREE)
        current = apply_local(before)
        for degree_step in range(2, DEGREE + 1):
            following = 2.0 * apply_local(current) - before
            before, current = (current, following)
        filtered = current[DEGREE : DEGREE + rows_here]
        gram_sum = lax.psum(inner_modes(filtered, filtered), "rows") / pixels
        factor_low = jnp.linalg.cholesky(gram_sum)
        mixing = lax.linalg.triangular_solve(
            factor_low, turnings[sweep], left_side=True, lower=True, transpose_a=True
        )
        picker = (sequence[sweep][None, :] == jnp.arange(nmodes, dtype=jnp.int32)[:, None]).astype(
            jnp.float32
        )
        mixing = jnp.dot(mixing, picker, precision=lax.Precision.HIGHEST)
        subspace = jnp.einsum("rcm,mn->rcn", filtered, mixing, precision=lax.Precision.HIGHEST)
    earlier = from_behind(subspace, "cuts", 1)
    earlier = jnp.where(lax.axis_index("cuts") == 0, start_modes[0], earlier)
    applied = apply_edge(subspace, section)
    coupling_term = inner_modes(earlier, subspace)
    rayleigh_term = inner_modes(subspace, applied)
    share_rows = nmodes // tiles
    coupling_sum, rayleigh_sum = lax.psum((coupling_term, rayleigh_term), "rows")
    coupling_part = lax.dynamic_slice_in_dim(
        coupling_sum, lax.axis_index("rows") * share_rows, share_rows, 0
    )
    rayleigh_part = lax.dynamic_slice_in_dim(
        rayleigh_sum, lax.axis_index("rows") * share_rows, share_rows, 0
    )
    return (subspace[None], (coupling_part / pixels)[None], (rayleigh_part / pixels)[None])


def solution(mesh):
    placed = (
        P("cuts", "rows", None, None),
        P("cuts", "rows", None),
        P("cuts", None, None, None),
        P("cuts", None, None),
    )
    return jax.shard_map(
        body,
        mesh=mesh,
        in_specs=placed,
        out_specs=(P("cuts", "rows", None, None), P("cuts", "rows", None), P("cuts", "rows", None)),
        check_vma=False,
    )
```

profile of v0, /device:TPU:8, one launch (start us, length us, event | category | flops | bytes accessed | tf_op | source)
XLA Modules:
  0.0 448.9 jit_solution(6304230805131383144)
XLA Ops:
  7.2 2.8 collective-permute-start.3
  10.0 1.9 collective-permute-start.2
  11.9 4.5 %collective-permute-start.1 = (f32[4,512]{1,0:T(4,128)}, f32[4,512]{1,0:T(4,128)S(1)}, u32[]{:S(2)}, u32[]{:S(2)}) collective-permute-start(f32[4,512]{1,0:T(4,128)} %bitcast.65), channel_id=1, source_target_pairs={{1,0},{2,1},{3,2},{4,3},{5,4},{6,5},{7,6},{8,7},{9,8},{10,9},{11,1... | collective-permute-start | bytes 24584 | tf_op jit(solution)/shard_map/ppermute | solution.py:18
  16.5 1.9 collective-permute-start
  18.4 4.2 collective-permute-done.1
  22.6 4.8 %collective-permute-done = f32[4,512]{1,0:T(4,128)S(1)} collective-permute-done((f32[4,512]{1,0:T(4,128)}, f32[4,512]{1,0:T(4,128)S(1)}, u32[]{:S(2)}, u32[]{:S(2)}) %collective-permute-start) | collective-permute-done | bytes 8224 | tf_op jit(solution)/shard_map/ppermute | solution.py:15
  27.4 0.7 pad_maximum_fusion.5
  28.1 1.4 pad_maximum_fusion
  29.6 2.0 fusion.7
  31.5 2.7 fusion.17
  34.2 4.0 fusion.27
  38.2 2.1 fusion.37
  40.3 2.4 convolution_bitcast_fusion.1
  43.1 97.2 %all-reduce.22.cloned.1.call-done = f32[128,128]{0,1:T(8,128)} async-done(((f32[128,128]{0,1:T(8,128)}), f32[128,128]{0,1:T(8,128)}) %all-reduce.22.cloned.1.call-update) | async-done | bytes 65552 | tf_op jit(solution)/shard_map/psum | solution.py:83
  140.3 0.8 broadcast_multiply_fusion.1
  141.2 0.9 fusion.108
  142.1 11.7 %cholesky.44 = f32[128,128]{1,0:T(8,128)S(1)} custom-call(f32[128,128]{1,0:T(8,128)S(1)} %fusion.108), custom_call_target="Cholesky" | custom-call | tf_op jit(solution)/shard_map/jit(cholesky)/cholesky | solution.py:84
  153.8 0.6 compare_reduce_fusion.1
  154.4 0.7 fusion.99
  155.1 9.8 %custom-call.6 = f32[1,128,128]{1,2,0:T(8,128)S(1)} custom-call(f32[1,128,128]{2,1,0:T(8,128)S(1)} %fusion.99), custom_call_target="InvertDiagBlocksLowerTriangular" | custom-call | tf_op jit(solution)/shard_map/triangular_solve/custom-call.0 | solution.py:85
  165.3 1.0 fusion.120
  166.3 1.9 collective-permute-start.5
  168.2 2.6 collective-permute-start.4
  170.9 9.7 %collective-permute-done.5 = f32[4,512,128]{2,1,0:T(8,128)S(1)} collective-permute-done((f32[4,512,128]{2,1,0:T(8,128)S(1)}, f32[4,512,128]{2,1,0:T(8,128)S(1)}, u32[]{:S(2)}, u32[]{:S(2)}) %collective-permute-start.5) | collective-permute-done | bytes 1048608 | tf_op jit(solution)/shard_map/ppermute | solution.py:18
  180.6 4.8 %collective-permute-done.4 = f32[4,512,128]{2,1,0:T(8,128)S(1)} collective-permute-done((f32[4,512,128]{2,1,0:T(8,128)S(1)}, f32[4,512,128]{2,1,0:T(8,128)S(1)}, u32[]{:S(2)}, u32[]{:S(2)}) %collective-permute-start.4) | collective-permute-done | bytes 1048608 | tf_op jit(solution)/shard_map/ppermute | solution.py:15
  185.6 2.0 fusion.45
  187.6 2.7 fusion.55
  190.2 4.0 fusion.65
  194.3 2.1 fusion.75
  196.4 2.4 convolution_bitcast_fusion
  198.9 96.1 %all-reduce.24.cloned.1.call-done = f32[128,128]{0,1:T(8,128)} async-done(((f32[128,128]{0,1:T(8,128)}), f32[128,128]{0,1:T(8,128)}) %all-reduce.24.cloned.1.call-update) | async-done | bytes 65552 | tf_op jit(solution)/shard_map/psum | solution.py:83
  295.1 0.8 broadcast_multiply_fusion
  296.0 0.9 fusion.104
  296.9 11.7 %cholesky.55 = f32[128,128]{1,0:T(8,128)S(1)} custom-call(f32[128,128]{1,0:T(8,128)S(1)} %fusion.104), custom_call_target="Cholesky" | custom-call | tf_op jit(solution)/shard_map/jit(cholesky)/cholesky | solution.py:84
  309.3 0.7 fusion.100
  309.9 9.8 %custom-call.7 = f32[1,128,128]{1,2,0:T(8,128)S(1)} custom-call(f32[1,128,128]{2,1,0:T(8,128)S(1)} %fusion.100), custom_call_target="InvertDiagBlocksLowerTriangular" | custom-call | tf_op jit(solution)/shard_map/triangular_solve/custom-call.0 | solution.py:85
  320.1 1.9 fusion.121
  322.1 3.6 collective-permute-start.6
  325.6 1.1 fusion.119
  326.7 1.9 collective-permute-start.7
  328.6 2.7 collective-permute-start.8
  331.3 1.2 collective-permute-done.7
  332.6 4.7 %collective-permute-done.8 = f32[1,512,128]{2,1,0:T(8,128)S(1)} collective-permute-done((f32[1,512,128]{2,1,0:T(8,128)S(1)}, f32[1,512,128]{2,1,0:T(8,128)S(1)}, u32[]{:S(2)}, u32[]{:S(2)}) %collective-permute-start.8) | collective-permute-done | bytes 262176 | tf_op jit(solution)/shard_map/ppermute | solution.py:15
  337.2 6.2 %convolution_bitcast_fusion.2 = f32[128,128]{1,0:T(8,128)} fusion(f32[4,512,128]{2,1,0:T(8,128)} %fusion.121, f32[1,512,128]{2,1,0:T(8,128)S(1)} %collective-permute-done.8, f32[1,512,128]{2,1,0:T(8,128)S(1)} %collective-permute-done.7, f32[4,512]{1,0:T(4,128)S(1)} %bitcast.68), kind=kOutput, calls=%fused_computation.96 | convolution fusion | flops 405536768 | bytes 2695168 | tf_op jit(solution)/shard_map/rcm,rcn->mn/dot_general | solution.py:42
  343.4 1.7 collective-permute-done.6
  345.1 3.7 convolution_bitcast_fusion.3
  348.8 92.3 %all-reduce.26.cloned.1.call-done = (f32[128,128]{1,0:T(8,128)}, f32[128,128]{1,0:T(8,128)}) async-done(((f32[128,128]{1,0:T(8,128)}, f32[128,128]{1,0:T(8,128)}), (f32[128,128]{1,0:T(8,128)}, f32[128,128]{1,0:T(8,128)})) %all-reduce.26.cloned.1.call-update) | async-done | bytes 131088 | tf_op jit(solution)/shard_map/psum | solution.py:99
  441.1 1.3 multiply_bitcast_fusion
  (30 shorter events, 2.3 us)
Async XLA Ops:
  7.2 133.1 %all-reduce.22.cloned.1.call-start = ((), (), s32[]{:S(2)}) async-start(), calls=%async_computation | async-start | bytes 131072 | tf_op jit(solution)/shard_map/psum | solution.py:83
  7.2 20.9 %collective-permute-start.3 = (f32[4,512,128]{2,1,0:T(8,128)}, f32[4,512,128]{2,1,0:T(8,128)S(1)}, u32[]{:S(2)}, u32[]{:S(2)}) collective-permute-start(f32[4,512,128]{2,1,0:T(8,128)} %bitcast.61), channel_id=1, source_target_pairs={{1,0},{2,1},{3,2},{4,3},{5,4},{6,5},{7,6},{8,7},{9,8},{10,9},{11,1... | collective-permute-start | bytes 3145736 | tf_op jit(solution)/shard_map/ppermute | solution.py:18
  10.0 18.1 %collective-permute-start.2 = (f32[4,512,128]{2,1,0:T(8,128)}, f32[4,512,128]{2,1,0:T(8,128)S(1)}, u32[]{:S(2)}, u32[]{:S(2)}) collective-permute-start(f32[4,512,128]{2,1,0:T(8,128)} %bitcast.62), channel_id=1, source_target_pairs={{0,1},{1,2},{2,3},{3,4},{4,5},{5,6},{6,7},{7,8},{8,9},{9,10},{10,1... | collective-permute-start | bytes 3145736 | tf_op jit(solution)/shard_map/ppermute | solution.py:15
  11.9 10.7 %collective-permute-start.1 = (f32[4,512]{1,0:T(4,128)}, f32[4,512]{1,0:T(4,128)S(1)}, u32[]{:S(2)}, u32[]{:S(2)}) collective-permute-start(f32[4,512]{1,0:T(4,128)} %bitcast.65), channel_id=1, source_target_pairs={{1,0},{2,1},{3,2},{4,3},{5,4},{6,5},{7,6},{8,7},{9,8},{10,9},{11,1... | collective-permute-start | bytes 24584 | tf_op jit(solution)/shard_map/ppermute | solution.py:18
  16.5 10.9 %collective-permute-start = (f32[4,512]{1,0:T(4,128)}, f32[4,512]{1,0:T(4,128)S(1)}, u32[]{:S(2)}, u32[]{:S(2)}) collective-permute-start(f32[4,512]{1,0:T(4,128)} %bitcast.66), channel_id=1, source_target_pairs={{0,1},{1,2},{2,3},{3,4},{4,5},{5,6},{6,7},{7,8},{8,9},{9,10},{10,1... | collective-permute-start | bytes 24584 | tf_op jit(solution)/shard_map/ppermute | solution.py:15
  29.6 2.0 copy-start
  40.3 2.7 copy-start.4
  40.3 124.6 %copy-start.2 = (f32[1,2,128,128]{3,2,1,0:T(8,128)S(1)}, f32[1,2,128,128]{3,2,1,0:T(8,128)}, u32[]{:S(2)}) copy-start(f32[1,2,128,128]{3,2,1,0:T(8,128)} %param.9) | copy-start | bytes 393220
  42.8 252.3 %all-reduce.24.cloned.1.call-start = ((), (), s32[]{:S(2)}) async-start(), calls=%async_computation.1 | async-start | bytes 131072 | tf_op jit(solution)/shard_map/psum | solution.py:83
  166.3 14.3 %collective-permute-start.5 = (f32[4,512,128]{2,1,0:T(8,128)S(1)}, f32[4,512,128]{2,1,0:T(8,128)S(1)}, u32[]{:S(2)}, u32[]{:S(2)}) collective-permute-start(f32[4,512,128]{2,1,0:T(8,128)S(1)} %fusion.120), channel_id=1, source_target_pairs={{1,0},{2,1},{3,2},{4,3},{5,4},{6,5},{7,6},{8,7},{9,8},{10,9},{11,1... | collective-permute-start | bytes 3145736 | tf_op jit(solution)/shard_map/ppermute | solution.py:18
  168.2 17.1 %collective-permute-start.4 = (f32[4,512,128]{2,1,0:T(8,128)S(1)}, f32[4,512,128]{2,1,0:T(8,128)S(1)}, u32[]{:S(2)}, u32[]{:S(2)}) collective-permute-start(f32[4,512,128]{2,1,0:T(8,128)S(1)} %fusion.120), channel_id=1, source_target_pairs={{0,1},{1,2},{2,3},{3,4},{4,5},{5,6},{6,7},{7,8},{8,9},{9,10},{10,1... | collective-permute-start | bytes 3145736 | tf_op jit(solution)/shard_map/ppermute | solution.py:15
  196.4 140.8 %copy-start.3 = (f32[1,4,512]{2,1,0:T(4,128)S(1)}, f32[1,4,512]{2,1,0:T(4,128)}, u32[]{:S(2)}) copy-start(f32[1,4,512]{2,1,0:T(4,128)} %param.8) | copy-start | bytes 24580
  198.9 242.2 %all-reduce.26.cloned.1.call-start = ((), (), s32[]{:S(2)}) async-start(), calls=%async_computation.2 | async-start | bytes 262144 | tf_op jit(solution)/shard_map/psum | solution.py:99
  322.1 23.0 %copy-start.1 = (f32[1,4,512,128]{3,2,1,0:T(8,128)S(1)}, f32[1,4,512,128]{3,2,1,0:T(8,128)}, u32[]{:S(2)}) copy-start(f32[1,4,512,128]{3,2,1,0:T(8,128)} %param.7) | copy-start | bytes 3145732
  322.1 23.0 %collective-permute-start.6 = (f32[4,512,128]{2,1,0:T(8,128)}, f32[4,512,128]{2,1,0:T(8,128)S(1)}, u32[]{:S(2)}, u32[]{:S(2)}) collective-permute-start(f32[4,512,128]{2,1,0:T(8,128)} %fusion.121), channel_id=1, source_target_pairs={{0,16},{1,17},{2,18},{3,19},{4,20},{5,21},{6,22},{7,23},{8,24},{9,... | collective-permute-start | bytes 3145736 | tf_op jit(solution)/shard_map/ppermute | solution.py:26
  326.7 5.8 %collective-permute-start.7 = (f32[1,512,128]{2,1,0:T(8,128)S(1)}, f32[1,512,128]{2,1,0:T(8,128)S(1)}, u32[]{:S(2)}, u32[]{:S(2)}) collective-permute-start(f32[1,512,128]{2,1,0:T(8,128)S(1)} %get-tuple-element.7), channel_id=1, source_target_pairs={{1,0},{2,1},{3,2},{4,3},{5,4},{6,5},{7,6},{8,7},{9,8},{10,9},{11,1... | collective-permute-start | bytes 786440 | tf_op jit(solution)/shard_map/ppermute | solution.py:18
  328.6 8.6 %collective-permute-start.8 = (f32[1,512,128]{2,1,0:T(8,128)S(1)}, f32[1,512,128]{2,1,0:T(8,128)S(1)}, u32[]{:S(2)}, u32[]{:S(2)}) collective-permute-start(f32[1,512,128]{2,1,0:T(8,128)S(1)} %get-tuple-element.8), channel_id=1, source_target_pairs={{0,1},{1,2},{2,3},{3,4},{4,5},{5,6},{6,7},{7,8},{8,9},{9,10},{10,1... | collective-permute-start | bytes 786440 | tf_op jit(solution)/shard_map/ppermute | solution.py:15
Sparse Core Ops, SparseCore 0:
  42.9 97.2 all-reduce.21
  199.0 96.0 all-reduce.23
  348.9 92.1 all-reduce.25
where the time goes:
time: 450 us; the launch traced here: 449 us
  waiting for transfers between devices  317 us (70%)
  other arithmetic  74.2 us (16%)
  starting transfers between devices  24.1 us (5%)
  matrix products  18.5 us (4%)
  between operations  14.1 us (3%)
    psum x2, waiting for transfers between devices, body(): gram_sum = lax.psum(inner_modes(filtered, filtered), 'rows') / pixels  193 us
    psum x1, waiting for transfers between devices, body(): lax.psum((coupling_term, rayleigh_term), 'rows')  92.3 us
    another operation x6, other arithmetic, body(): factor_low = jnp.linalg.cholesky(gram_sum)  24.8 us
    another operation x4, other arithmetic, body(): lax.linalg.triangular_solve(factor_low, turnings[sweep], left_side=True,...  20.9 us
    sub x6, other arithmetic, body(): following = 2.0 * apply_local(current) - before  17.6 us
    ppermute x4, waiting for transfers between devices, padded_2(): lax.ppermute(lax.slice_in_dim(block, 0, width, axis=dim), axis, backward)  15.2 us
    dot_general x4, matrix products, inner_modes(): jnp.einsum('rcm,rcn->mn', left, right, precision=lax.Precision.HIGHEST)  14.8 us
    ppermute x4, waiting for transfers between devices, padded_2(): lax.ppermute(lax.slice_in_dim(block, block.shape[dim] - width, None, axis...  14.2 us
  transfers between devices with their start and end apart: 12, of which 10 were waited for; matrix products, arithmetic and copies ran while one was open for 2% of the time, Pallas kernels for 0%

commit v1 on v0

--- a/solution.py
+++ b/solution.py
@@ -2,6 +2,7 @@
 import jax.numpy as jnp
 from jax import lax
 from jax.sharding import PartitionSpec as P
+from jax.lax import all_gather
 
 DEGREE = 4
 ITERS = 2
@@ -80,7 +81,12 @@
             following = 2.0 * apply_local(current) - before
             before, current = (current, following)
         filtered = current[DEGREE : DEGREE + rows_here]
-        gram_sum = lax.psum(inner_modes(filtered, filtered), "rows") / pixels
+
+        def begin_sums_all(values):
+            taken_in = all_gather(values, "rows").sum(axis=0)
+            return taken_in
+
+        gram_sum = begin_sums_all(inner_modes(filtered, filtered)) / pixels
         factor_low = jnp.linalg.cholesky(gram_sum)
         mixing = lax.linalg.triangular_solve(
             factor_low, turnings[sweep], left_side=True, lower=True, transpose_a=True

time: 450 us -> 350 us (0.78)
  waiting for transfers between devices: 317 us -> 217 us
    psum x2 -> x0, waiting for transfers between devices: 193 us -> none  [body(): gram_sum = lax.psum(inner_modes(filtered, filtered), 'rows') / pixels]
    all_gather x0 -> x2, waiting for transfers between devices: none -> 89.7 us  [begin_sums_all(): taken_in = all_gather(values, 'rows').sum(axis=0)]
where the time goes in v1:
time: 350 us; the launch traced here: 349 us
  waiting for transfers between devices  217 us (62%)
  other arithmetic  73.4 us (21%)
  starting transfers between devices  25.1 us (7%)
  matrix products  18.4 us (5%)
  between operations  14.1 us (4%)
    psum x1, waiting for transfers between devices, body(): lax.psum((coupling_term, rayleigh_term), 'rows')  92 us
    all_gather x2, waiting for transfers between devices, begin_sums_all(): taken_in = all_gather(values, 'rows').sum(axis=0)  89.7 us
    another operation x6, other arithmetic, body(): factor_low = jnp.linalg.cholesky(gram_sum)  24.8 us
    another operation x4, other arithmetic, body(): lax.linalg.triangular_solve(factor_low, turnings[sweep], left_side=True,...  20.9 us
    sub x6, other arithmetic, body(): following = 2.0 * apply_local(current) - before  17.6 us
    ppermute x4, waiting for transfers between devices, padded_2(): lax.ppermute(lax.slice_in_dim(block, 0, width, axis=dim), axis, backward)  16.3 us
    dot_general x4, matrix products, inner_modes(): jnp.einsum('rcm,rcn->mn', left, right, precision=lax.Precision.HIGHEST)  14.7 us
    ppermute x4, waiting for transfers between devices, padded_2(): lax.ppermute(lax.slice_in_dim(block, block.shape[dim] - width, None, axis...  14.3 us
  transfers between devices with their start and end apart: 12, of which 10 were waited for; matrix products, arithmetic and copies ran while one was open for 2% of the time, Pallas kernels for 0%

profile of v1, /device:TPU:8, one launch (start us, length us, event | category | flops | bytes accessed | tf_op | source)
XLA Modules:
  0.0 349.3 jit_solution(14084883820328481354)
XLA Ops:
  7.2 2.8 collective-permute-start.3
  10.0 1.9 collective-permute-start.2
  11.9 4.5 %collective-permute-start.1 = (f32[4,512]{1,0:T(4,128)}, f32[4,512]{1,0:T(4,128)S(1)}, u32[]{:S(2)}, u32[]{:S(2)}) collective-permute-start(f32[4,512]{1,0:T(4,128)} %bitcast.69), channel_id=1, source_target_pairs={{1,0},{2,1},{3,2},{4,3},{5,4},{6,5},{7,6},{8,7},{9,8},{10,9},{11,1... | collective-permute-start | bytes 24584 | tf_op jit(solution)/shard_map/ppermute | solution.py:19
  16.5 1.9 collective-permute-start
  18.4 4.2 %collective-permute-done.1 = f32[4,512]{1,0:T(4,128)S(1)} collective-permute-done((f32[4,512]{1,0:T(4,128)}, f32[4,512]{1,0:T(4,128)S(1)}, u32[]{:S(2)}, u32[]{:S(2)}) %collective-permute-start.1) | collective-permute-done | bytes 8224 | tf_op jit(solution)/shard_map/ppermute | solution.py:19
  22.6 4.8 %collective-permute-done = f32[4,512]{1,0:T(4,128)S(1)} collective-permute-done((f32[4,512]{1,0:T(4,128)}, f32[4,512]{1,0:T(4,128)S(1)}, u32[]{:S(2)}, u32[]{:S(2)}) %collective-permute-start) | collective-permute-done | bytes 8224 | tf_op jit(solution)/shard_map/ppermute | solution.py:16
  27.4 0.7 pad_maximum_fusion.5
  28.1 1.4 pad_maximum_fusion
  29.6 2.0 fusion.7
  31.5 2.7 fusion.17
  34.2 4.0 %fusion.27 = f32[12,512,128]{2,1,0:T(8,128)S(1)} fusion(f32[12,512,128]{2,1,0:T(8,128)S(1)} %fusion.17, f32[12]{0:T(128)S(1)} %and_convert_fusion, f32[12,512]{1,0:T(8,128)S(1)} %pad_maximum_fusion.5, f32[12,512,128]{2,1,0:T(8,128)S(1)} %pad_maximum_fusion), kind=kLoop, calls=%fused_computation.43 | loop fusion | flops 17301504 | bytes 9461808 | tf_op jit(solution)/shard_map/sub | solution.py:81
  38.2 2.1 fusion.37
  40.3 2.5 convolution_bitcast_fusion.1
  42.8 0.2 all-gather.7.cloned.1.call-start
  43.1 45.4 %all-gather.5.cloned.1.call-done = f32[2048,128]{1,0:T(8,128)} async-done(((f32[128,128]{1,0:T(8,128)}), f32[2048,128]{1,0:T(8,128)}) %all-gather.5.cloned.1.call-update) | async-done | bytes 1048592 | tf_op jit(solution)/shard_map/all_gather | solution.py:86
  88.4 1.3 reduce_sum.18
  90.0 11.7 %cholesky.44 = f32[128,128]{1,0:T(8,128)S(1)} custom-call(f32[128,128]{1,0:T(8,128)S(1)} %fusion.108), custom_call_target="Cholesky" | custom-call | tf_op jit(solution)/shard_map/jit(cholesky)/cholesky | solution.py:90
  101.7 0.6 compare_reduce_fusion.1
  102.4 0.7 fusion.99
  103.0 9.8 %custom-call.6 = f32[1,128,128]{1,2,0:T(8,128)S(1)} custom-call(f32[1,128,128]{2,1,0:T(8,128)S(1)} %fusion.99), custom_call_target="InvertDiagBlocksLowerTriangular" | custom-call | tf_op jit(solution)/shard_map/triangular_solve/custom-call.0 | solution.py:91
  113.2 1.0 fusion.120
  114.2 3.2 collective-permute-start.5
  117.4 2.1 collective-permute-start.4
  119.6 10.2 %collective-permute-done.5 = f32[4,512,128]{2,1,0:T(8,128)S(1)} collective-permute-done((f32[4,512,128]{2,1,0:T(8,128)S(1)}, f32[4,512,128]{2,1,0:T(8,128)S(1)}, u32[]{:S(2)}, u32[]{:S(2)}) %collective-permute-start.5) | collective-permute-done | bytes 1048608 | tf_op jit(solution)/shard_map/ppermute | solution.py:19
  129.8 4.8 %collective-permute-done.4 = f32[4,512,128]{2,1,0:T(8,128)S(1)} collective-permute-done((f32[4,512,128]{2,1,0:T(8,128)S(1)}, f32[4,512,128]{2,1,0:T(8,128)S(1)}, u32[]{:S(2)}, u32[]{:S(2)}) %collective-permute-start.4) | collective-permute-done | bytes 1048608 | tf_op jit(solution)/shard_map/ppermute | solution.py:16
  134.8 2.0 fusion.45
  136.7 2.7 fusion.55
  139.4 4.0 %fusion.65 = f32[12,512,128]{2,1,0:T(8,128)S(1)} fusion(f32[12,512,128]{2,1,0:T(8,128)S(1)} %fusion.55, f32[12]{0:T(128)S(1)} %and_convert_fusion, f32[12,512]{1,0:T(8,128)S(1)} %pad_maximum_fusion.5, f32[12,512,128]{2,1,0:T(8,128)S(1)} %pad_maximum_fusion.1), kind=kLoop, calls=%fused_computation.81 | loop fusion | flops 17301504 | bytes 9461808 | tf_op jit(solution)/shard_map/sub | solution.py:81
  143.4 2.1 fusion.75
  145.6 2.5 convolution_bitcast_fusion
  148.1 44.4 %all-gather.7.cloned.1.call-done = f32[2048,128]{1,0:T(8,128)} async-done(((f32[128,128]{1,0:T(8,128)}), f32[2048,128]{1,0:T(8,128)}) %all-gather.7.cloned.1.call-update) | async-done | bytes 1048592 | tf_op jit(solution)/shard_map/all_gather | solution.py:86
  192.4 1.3 reduce_sum.19
  194.0 11.7 %cholesky.55 = f32[128,128]{1,0:T(8,128)S(1)} custom-call(f32[128,128]{1,0:T(8,128)S(1)} %fusion.104), custom_call_target="Cholesky" | custom-call | tf_op jit(solution)/shard_map/jit(cholesky)/cholesky | solution.py:90
  205.7 0.6 compare_reduce_fusion
  206.3 0.7 fusion.100
  207.0 9.8 %custom-call.7 = f32[1,128,128]{1,2,0:T(8,128)S(1)} custom-call(f32[1,128,128]{2,1,0:T(8,128)S(1)} %fusion.100), custom_call_target="InvertDiagBlocksLowerTriangular" | custom-call | tf_op jit(solution)/shard_map/triangular_solve/custom-call.0 | solution.py:91
  217.2 1.9 fusion.121
  219.2 3.6 %collective-permute-start.6 = (f32[4,512,128]{2,1,0:T(8,128)}, f32[4,512,128]{2,1,0:T(8,128)S(1)}, u32[]{:S(2)}, u32[]{:S(2)}) collective-permute-start(f32[4,512,128]{2,1,0:T(8,128)} %fusion.121), channel_id=1, source_target_pairs={{0,16},{1,17},{2,18},{3,19},{4,20},{5,21},{6,22},{7,23},{8,24},{9,... | collective-permute-start | bytes 3145736 | tf_op jit(solution)/shard_map/ppermute | solution.py:27
  222.7 1.1 fusion.119
  223.8 2.9 collective-permute-start.7
  226.7 1.9 collective-permute-start.8
  228.6 1.9 collective-permute-done.7
  230.6 4.7 %collective-permute-done.8 = f32[1,512,128]{2,1,0:T(8,128)S(1)} collective-permute-done((f32[1,512,128]{2,1,0:T(8,128)S(1)}, f32[1,512,128]{2,1,0:T(8,128)S(1)}, u32[]{:S(2)}, u32[]{:S(2)}) %collective-permute-start.8) | collective-permute-done | bytes 262176 | tf_op jit(solution)/shard_map/ppermute | solution.py:16
  235.3 6.2 %convolution_bitcast_fusion.2 = f32[128,128]{1,0:T(8,128)} fusion(f32[4,512,128]{2,1,0:T(8,128)} %fusion.121, f32[1,512,128]{2,1,0:T(8,128)S(1)} %collective-permute-done.8, f32[1,512,128]{2,1,0:T(8,128)S(1)} %collective-permute-done.7, f32[4,512]{1,0:T(4,128)S(1)} %bitcast.72), kind=kOutput, calls=%fused_computation.96 | convolution fusion | flops 405536768 | bytes 2695168 | tf_op jit(solution)/shard_map/rcm,rcn->mn/dot_general | solution.py:43
  241.5 4.3 %collective-permute-done.6 = f32[4,512,128]{2,1,0:T(8,128)S(1)} collective-permute-done((f32[4,512,128]{2,1,0:T(8,128)}, f32[4,512,128]{2,1,0:T(8,128)S(1)}, u32[]{:S(2)}, u32[]{:S(2)}) %collective-permute-start.6) | collective-permute-done | bytes 1048608 | tf_op jit(solution)/shard_map/ppermute | solution.py:27
  245.8 3.7 %convolution_bitcast_fusion.3 = f32[128,128]{1,0:T(8,128)} fusion(f32[4,512,128]{2,1,0:T(8,128)} %fusion.121, f32[4,512,128]{2,1,0:T(8,128)S(1)} %collective-permute-done.6, pred[]{:T(512)S(6)} %eq.41, f32[1,4,512,128]{3,2,1,0:T(8,128)S(1)} %copy-done.1), kind=kOutput, calls=%fused_computation.97 | convolution fusion | flops 402915328 | bytes 3211265 | tf_op jit(solution)/shard_map/rcm,rcn->mn/dot_general | solution.py:43
  249.5 92.0 %all-reduce.20.cloned.1.call-done = (f32[128,128]{1,0:T(8,128)}, f32[128,128]{1,0:T(8,128)}) async-done(((f32[128,128]{1,0:T(8,128)}, f32[128,128]{1,0:T(8,128)}), (f32[128,128]{1,0:T(8,128)}, f32[128,128]{1,0:T(8,128)})) %all-reduce.20.cloned.1.call-update) | async-done | bytes 131088 | tf_op jit(solution)/shard_map/psum | solution.py:105
  341.5 1.3 multiply_bitcast_fusion
  (34 shorter events, 1.6 us)
Async XLA Ops:
  7.2 81.3 %all-gather.5.cloned.1.call-start = ((), (), s32[]{:S(2)}) async-start(), calls=%async_computation | async-start | bytes 1114112 | tf_op jit(solution)/shard_map/all_gather | solution.py:86
  7.2 20.9 %collective-permute-start.3 = (f32[4,512,128]{2,1,0:T(8,128)}, f32[4,512,128]{2,1,0:T(8,128)S(1)}, u32[]{:S(2)}, u32[]{:S(2)}) collective-permute-start(f32[4,512,128]{2,1,0:T(8,128)} %bitcast.63), channel_id=1, source_target_pairs={{1,0},{2,1},{3,2},{4,3},{5,4},{6,5},{7,6},{8,7},{9,8},{10,9},{11,1... | collective-permute-start | bytes 3145736 | tf_op jit(solution)/shard_map/ppermute | solution.py:19
  10.0 18.1 %collective-permute-start.2 = (f32[4,512,128]{2,1,0:T(8,128)}, f32[4,512,128]{2,1,0:T(8,128)S(1)}, u32[]{:S(2)}, u32[]{:S(2)}) collective-permute-start(f32[4,512,128]{2,1,0:T(8,128)} %bitcast.64), channel_id=1, source_target_pairs={{0,1},{1,2},{2,3},{3,4},{4,5},{5,6},{6,7},{7,8},{8,9},{9,10},{10,1... | collective-permute-start | bytes 3145736 | tf_op jit(solution)/shard_map/ppermute | solution.py:16
  11.9 10.7 %collective-permute-start.1 = (f32[4,512]{1,0:T(4,128)}, f32[4,512]{1,0:T(4,128)S(1)}, u32[]{:S(2)}, u32[]{:S(2)}) collective-permute-start(f32[4,512]{1,0:T(4,128)} %bitcast.69), channel_id=1, source_target_pairs={{1,0},{2,1},{3,2},{4,3},{5,4},{6,5},{7,6},{8,7},{9,8},{10,9},{11,1... | collective-permute-start | bytes 24584 | tf_op jit(solution)/shard_map/ppermute | solution.py:19
  16.5 10.9 %collective-permute-start = (f32[4,512]{1,0:T(4,128)}, f32[4,512]{1,0:T(4,128)S(1)}, u32[]{:S(2)}, u32[]{:S(2)}) collective-permute-start(f32[4,512]{1,0:T(4,128)} %bitcast.70), channel_id=1, source_target_pairs={{0,1},{1,2},{2,3},{3,4},{4,5},{5,6},{6,7},{7,8},{8,9},{9,10},{10,1... | collective-permute-start | bytes 24584 | tf_op jit(solution)/shard_map/ppermute | solution.py:16
  29.6 2.0 copy-start
  40.3 2.7 copy-start.4
  40.3 72.5 %copy-start.2 = (f32[1,2,128,128]{3,2,1,0:T(8,128)S(1)}, f32[1,2,128,128]{3,2,1,0:T(8,128)}, u32[]{:S(2)}) copy-start(f32[1,2,128,128]{3,2,1,0:T(8,128)} %param.9) | copy-start | bytes 393220
  42.8 149.6 %all-gather.7.cloned.1.call-start = ((), (), s32[]{:S(2)}) async-start(), calls=%async_computation.1 | async-start | bytes 1114112 | tf_op jit(solution)/shard_map/all_gather | solution.py:86
  114.2 15.5 %collective-permute-start.5 = (f32[4,512,128]{2,1,0:T(8,128)S(1)}, f32[4,512,128]{2,1,0:T(8,128)S(1)}, u32[]{:S(2)}, u32[]{:S(2)}) collective-permute-start(f32[4,512,128]{2,1,0:T(8,128)S(1)} %fusion.120), channel_id=1, source_target_pairs={{1,0},{2,1},{3,2},{4,3},{5,4},{6,5},{7,6},{8,7},{9,8},{10,9},{11,1... | collective-permute-start | bytes 3145736 | tf_op jit(solution)/shard_map/ppermute | solution.py:19
  117.4 17.1 %collective-permute-start.4 = (f32[4,512,128]{2,1,0:T(8,128)S(1)}, f32[4,512,128]{2,1,0:T(8,128)S(1)}, u32[]{:S(2)}, u32[]{:S(2)}) collective-permute-start(f32[4,512,128]{2,1,0:T(8,128)S(1)} %fusion.120), channel_id=1, source_target_pairs={{0,1},{1,2},{2,3},{3,4},{4,5},{5,6},{6,7},{7,8},{8,9},{9,10},{10,1... | collective-permute-start | bytes 3145736 | tf_op jit(solution)/shard_map/ppermute | solution.py:16
  148.0 87.3 %copy-start.3 = (f32[1,4,512]{2,1,0:T(4,128)S(1)}, f32[1,4,512]{2,1,0:T(4,128)}, u32[]{:S(2)}) copy-start(f32[1,4,512]{2,1,0:T(4,128)} %param.8) | copy-start | bytes 24580
  148.0 193.5 %all-reduce.20.cloned.1.call-start = ((), (), s32[]{:S(2)}) async-start(), calls=%async_computation.2 | async-start | bytes 262144 | tf_op jit(solution)/shard_map/psum | solution.py:105
  219.2 26.6 %copy-start.1 = (f32[1,4,512,128]{3,2,1,0:T(8,128)S(1)}, f32[1,4,512,128]{3,2,1,0:T(8,128)}, u32[]{:S(2)}) copy-start(f32[1,4,512,128]{3,2,1,0:T(8,128)} %param.7) | copy-start | bytes 3145732
  219.2 26.6 %collective-permute-start.6 = (f32[4,512,128]{2,1,0:T(8,128)}, f32[4,512,128]{2,1,0:T(8,128)S(1)}, u32[]{:S(2)}, u32[]{:S(2)}) collective-permute-start(f32[4,512,128]{2,1,0:T(8,128)} %fusion.121), channel_id=1, source_target_pairs={{0,16},{1,17},{2,18},{3,19},{4,20},{5,21},{6,22},{7,23},{8,24},{9,... | collective-permute-start | bytes 3145736 | tf_op jit(solution)/shard_map/ppermute | solution.py:27
  223.8 6.8 %collective-permute-start.7 = (f32[1,512,128]{2,1,0:T(8,128)S(1)}, f32[1,512,128]{2,1,0:T(8,128)S(1)}, u32[]{:S(2)}, u32[]{:S(2)}) collective-permute-start(f32[1,512,128]{2,1,0:T(8,128)S(1)} %get-tuple-element.7), channel_id=1, source_target_pairs={{1,0},{2,1},{3,2},{4,3},{5,4},{6,5},{7,6},{8,7},{9,8},{10,9},{11,1... | collective-permute-start | bytes 786440 | tf_op jit(solution)/shard_map/ppermute | solution.py:19
  226.7 8.6 %collective-permute-start.8 = (f32[1,512,128]{2,1,0:T(8,128)S(1)}, f32[1,512,128]{2,1,0:T(8,128)S(1)}, u32[]{:S(2)}, u32[]{:S(2)}) collective-permute-start(f32[1,512,128]{2,1,0:T(8,128)S(1)} %get-tuple-element.8), channel_id=1, source_target_pairs={{0,1},{1,2},{2,3},{3,4},{4,5},{5,6},{6,7},{7,8},{8,9},{9,10},{10,1... | collective-permute-start | bytes 786440 | tf_op jit(solution)/shard_map/ppermute | solution.py:16
Sparse Core Ops, SparseCore 0:
  42.9 45.4 all-gather.4
  148.2 44.2 all-gather.6
  249.6 91.8 all-reduce.19
